TPU v7x, 768 devices: a whole 4x8x12 slice. The times are simulated.
768 devices in a mesh: seq: 48 (over z, x), head: 16 (over y, core).
Axes of the slice: x: 4, y: 8, z: 12, core: 2. Of those that a mesh axis runs over, the one named last changes fastest.
Arguments:
- queries: bfloat16 [24576, 8192], P('seq', 'head'), may hold values from -0.5 to 0.5
- keys: bfloat16 [24576, 8192], P('seq', 'head'), may hold values from -6 to 6
- values: bfloat16 [24576, 8192], P('seq', 'head'), may hold values from -6 to 6
- cotangent: bfloat16 [24576, 8192], P('seq', 'head'), may hold values from -6 to 6
- log_decay: float32 [64, 24576], P('head', 'seq'), may hold values from -0.6 to 0
- starts: int32 [24576], P('seq'), may hold values 0 or 1
Outputs:
- attn_out: bfloat16 [24576, 8192], P('seq', 'head')
- grad_query: bfloat16 [24576, 8192], P('seq', 'head')
- grad_key: bfloat16 [24576, 8192], P('seq', 'head')
- grad_value: bfloat16 [24576, 8192], P('seq', 'head')
All inputs are finite; a program needn't handle non-finite values. No bound on the sum of `starts` on one device may be relied on, other than what follows from the above.
Results may differ from a plain program's by a relative error of at most 0.0095.
Values may be sent and summed in bfloat16 or wider, within the bound.
A program may use at most 64 MiB of HBM per device.

v0:
```python
import jax
import jax.numpy as jnp
from jax import lax
from jax.sharding import PartitionSpec as P

HEAD_TOTAL = 64
HEAD_DIM = 128


EPS = 1e-05


def prefix(part, axis, combine, identity):
    count = lax.axis_size(axis)
    place = lax.axis_index(axis)
    ahead = count - 1 - place
    gathered = jax.tree.map(lambda a: lax.all_gather(a, axis), part)
    state = jax.tree.map(lambda a, e: jnp.zeros_like(a) + jnp.asarray(e, a.dtype), part, identity)

    def one(lap, state):
        source = count - 1 - lap
        return combine(
            state, jax.tree.map(lambda a: lax.dynamic_index_in_dim(a, source, 0, False), gathered)
        )

    return lax.fori_loop(0, ahead, one, state)


def block_factors(log_rates, start_flags):
    cum_log = jnp.cumsum(log_rates, axis=1)
    doc_count = jnp.cumsum(start_flags)
    length = start_flags.shape[0]
    position = jnp.arange(length, dtype=jnp.int32)
    inside = (position[:, None] >= position[None, :]) & (doc_count[:, None] == doc_count[None, :])
    gap = cum_log[:, :, None] - cum_log[:, None, :]
    weight = jnp.where(inside[None], jnp.exp(jnp.minimum(gap, 0.0)), 0.0)
    entering = jnp.where(doc_count[None, :] == 0, jnp.exp(cum_log), 0.0)
    leaving = jnp.where(
        doc_count[None, :] == doc_count[-1], jnp.exp(cum_log[:, -1:] - cum_log), 0.0
    )
    carried = jnp.where(doc_count[-1] == 0, jnp.exp(cum_log[:, -1]), 0.0)
    return (weight, entering, leaving, carried)


def combine(earlier, later):
    return (earlier[0] * later[0], later[0][:, None, None] * earlier[1] + later[1])


def carry_factors(totals, my_index):
    shard_count = totals.shape[0]
    source = jnp.arange(shard_count, dtype=jnp.int32)[:, None]
    middle = jnp.arange(shard_count, dtype=jnp.int32)[None, :]
    between = (middle > source) & (middle < my_index)
    valid = source < my_index
    factor = jnp.prod(jnp.where(between[:, :, None], totals[None, :, :], 1.0), axis=1)
    return jnp.where(valid, factor, 0.0)


def per_device(queries, keys, values, cotangent, log_decay, starts):
    length, row_width = queries.shape
    head_count = log_decay.shape[0]
    head_dim = row_width // head_count
    full_width = HEAD_TOTAL * HEAD_DIM

    def by_head(array):
        return array.reshape(length, head_count, head_dim).transpose(1, 0, 2)

    def by_token(array):
        return array.transpose(1, 0, 2).reshape(length, row_width)

    query_heads = by_head(queries)
    key_heads = by_head(keys)
    value_heads = by_head(values)
    cotangent_heads = by_head(cotangent)

    def local_forward(pieces):
        query_head, key_head, value_head, log_rates = pieces
        weight, entering, leaving, carried = block_factors(log_rates[None], starts)
        scores = jnp.einsum("td,sd->ts", query_head, key_head, preferred_element_type=jnp.float32)
        weights_rounded = (scores * weight[0]).astype(jnp.bfloat16)
        intra_out = jnp.dot(weights_rounded, value_head, preferred_element_type=jnp.float32)
        keys_decayed = (leaving[0][:, None] * key_head).astype(jnp.bfloat16)
        update = jnp.einsum(
            "sd,se->de", keys_decayed, value_head, preferred_element_type=jnp.float32
        ).astype(jnp.bfloat16)
        return (weights_rounded, intra_out, update, entering[0], carried[0])

    weights_all, intra_out, update, entering, carried = lax.map(
        local_forward, (query_heads, key_heads, value_heads, log_decay)
    )
    unit_decay = jnp.ones((head_count,), jnp.float32)
    zero_state = jnp.zeros((head_count, head_dim, head_dim), jnp.float32)
    totals = lax.all_gather(carried[None, :], "seq", axis=0, tiled=True)
    factor = carry_factors(totals, lax.axis_index("seq"))
    prefix_state = jnp.sum(
        factor[:, :, None, None]
        * lax.all_gather(update[None], "seq", axis=0, tiled=True).astype(jnp.float32),
        axis=0,
    )
    state_rounded = prefix_state.astype(jnp.bfloat16)
    carried_out = jnp.einsum(
        "htd,hde->hte", query_heads, state_rounded, preferred_element_type=jnp.float32
    )
    outputs = intra_out + entering[:, :, None] * carried_out
    square_part = jnp.sum(outputs * outputs, axis=(0, 2))
    grad_part = jnp.sum(cotangent_heads * outputs, axis=(0, 2))
    square_sum = lax.psum(square_part, "head")
    inverse_scale = lax.rsqrt(square_sum / full_width + EPS)
    attn_heads = (outputs * inverse_scale[None, :, None]).astype(jnp.bfloat16)
    grad_sum = lax.psum(grad_part, "head")
    cubed = inverse_scale * inverse_scale * inverse_scale
    grad_out = (
        inverse_scale[None, :, None] * cotangent_heads
        - (cubed * grad_sum / full_width)[None, :, None] * outputs
    ).astype(jnp.bfloat16)
    queries_decayed = (entering[:, :, None] * query_heads).astype(jnp.bfloat16)
    grad_state = jnp.einsum(
        "htd,hte->hde", queries_decayed, grad_out, preferred_element_type=jnp.float32
    ).astype(jnp.bfloat16)
    decay_out, back_state = prefix(
        (carried, grad_state.astype(jnp.float32)), "seq", combine, (unit_decay, zero_state)
    )
    back_rounded = back_state.astype(jnp.bfloat16)

    def local_backward(pieces):
        (
            query_head,
            key_head,
            value_head,
            grad_head,
            log_rates,
            weights_rounded,
            state_head,
            back_head,
        ) = pieces
        weight, entering_one, leaving_one, carried_one = block_factors(log_rates[None], starts)
        grads_rounded = (
            jnp.einsum("td,sd->ts", grad_head, value_head, preferred_element_type=jnp.float32)
            * weight[0]
        ).astype(jnp.bfloat16)
        grad_query = jnp.dot(grads_rounded, key_head, preferred_element_type=jnp.float32)
        grad_query = grad_query + entering_one[0][:, None] * jnp.einsum(
            "te,de->td", grad_head, state_head, preferred_element_type=jnp.float32
        )
        grad_key = jnp.einsum(
            "ts,td->sd", grads_rounded, query_head, preferred_element_type=jnp.float32
        )
        grad_key = grad_key + leaving_one[0][:, None] * jnp.einsum(
            "se,de->sd", value_head, back_head, preferred_element_type=jnp.float32
        )
        grad_value = jnp.einsum(
            "ts,td->sd", weights_rounded, grad_head, preferred_element_type=jnp.float32
        )
        grad_value = grad_value + leaving_one[0][:, None] * jnp.einsum(
            "sd,de->se", key_head, back_head, preferred_element_type=jnp.float32
        )
        return (
            grad_query.astype(jnp.bfloat16),
            grad_key.astype(jnp.bfloat16),
            grad_value.astype(jnp.bfloat16),
        )

    grad_query, grad_key, grad_value = lax.map(
        local_backward,
        (
            query_heads,
            key_heads,
            value_heads,
            grad_out,
            log_decay,
            weights_all,
            state_rounded,
            back_rounded,
        ),
    )
    return (by_token(attn_heads), by_token(grad_query), by_token(grad_key), by_token(grad_value))


def solution(mesh):
    in_specs = (
        P("seq", "head"),
        P("seq", "head"),
        P("seq", "head"),
        P("seq", "head"),
        P("head", "seq"),
        P("seq"),
    )
    out_specs = (P("seq", "head"), P("seq", "head"), P("seq", "head"), P("seq", "head"))
    return jax.shard_map(
        per_device, mesh=mesh, in_specs=in_specs, out_specs=out_specs, check_vma=False
    )
```

profile of v0, /device:TPU:1, one launch (start us, length us, event | category | flops | bytes accessed | tf_op | source)
XLA Modules:
  0.0 458.9 jit_solution(1446715537004562332)
XLA Ops:
  8.5 1.3 copy.64
  11.1 32.6 %while.50 = (s32[]{:T(128)}, bf16[4,512,512]{2,1,0:T(8,128)(2,1)}, f32[4,512,128]{1,2,0:T(8,128)}, bf16[4,128,128]{2,1,0:T(8,128)(2,1)}, f32[4,512]{1,0:T(4,128)...) while((s32[]{:T(128)}, bf16[4,512,512]{2,1,0:T(8,128)(2,1)}, ...), condition=%wide.region_5.6_spmd, body=%wide.region_2.5_spmd.sunk | while | flops 153374736 | bytes 2575779 | solution.py:88
  13.2 1.4 exponential_select_fusion.6
  14.6 1.2 bitcast_dynamic-update-slice_fusion.2
  21.4 1.4 exponential_select_fusion.6
  22.8 1.2 bitcast_dynamic-update-slice_fusion.2
  29.6 1.4 exponential_select_fusion.6
  30.9 1.2 bitcast_dynamic-update-slice_fusion.2
  37.7 1.4 exponential_select_fusion.6
  39.0 1.2 bitcast_dynamic-update-slice_fusion.2
  43.8 1.3 dynamic-slice
  46.0 99.0 %all-reduce = f32[192]{0:T(256)S(1)} all-reduce(f32[192]{0:T(256)S(1)} %dynamic-update-slice), channel_id=2, replica_groups=mesh['seq'=48,'head'=16] {'seq'}, use_global_device_ids=true, to_apply=%add | all-reduce | flops 192 | bytes 1536
  145.5 1.3 copy.76
  146.7 25.4 %all-gather.6.cloned.1.call-done = bf16[192,128,128]{2,1,0:T(8,128)(2,1)} async-done(((bf16[4,128,128]{2,1,0:T(8,128)(2,1)}), bf16[192,128,128]{2,1,0:T(8,128)(2,1)}) %all-gather.6.cloned.1.call-update) | async-done | bytes 6291472 | tf_op jit(solution)/shard_map/all_gather | solution.py:97
  172.1 4.2 fusion.69
  176.3 1.4 multiply_reduce_fusion
  177.7 29.6 %all-reduce.1 = (f32[512]{0:T(512)S(1)}, f32[512]{0:T(512)S(1)}) all-reduce(f32[512]{0:T(512)S(1)} %get-tuple-element.510, f32[512]{0:T(512)S(1)} %get-tuple-element.509), channel_id=1, replica_groups=mesh['seq'=48,'head'=16] {'head'}, use_global_device_ids=true, to_apply=%region_9.10 | all-reduce | flops 1024 | bytes 8192 | tf_op jit(solution)/shard_map/psum | solution.py:107
  207.4 2.3 subtract_convert_fusion
  210.7 2.0 copy.86
  212.8 146.9 %all-gather.8.cloned.1.call-done = f32[192,128,128]{2,1,0:T(8,128)} async-done(((f32[4,128,128]{2,1,0:T(8,128)}), f32[192,128,128]{2,1,0:T(8,128)}) %all-gather.8.cloned.1.call-update) | async-done | bytes 12582928 | tf_op jit(solution)/shard_map/all_gather | solution.py:17
  359.7 52.0 %while.51 = (s32[]{:T(128)}, f32[4,128,128]{2,1,0:T(8,128)S(1)}, s32[]{:T(128)}, f32[48,4]{1,0:T(8,128)S(1)}, f32[48,4,128,128]{3,2,1,0:T(8,128)}, /*index=5*/s32[]{:T(128)}, s32[]{:T(128)}, s32[]{:T(128)}, s32[]{:T(128)}) while((s32[]{:T(128)}, f32[4,128,128]{2,1,0:T(8,128)S(1)}, s32[]{:T(128)}, f32[48,4]{1,0:T(8,128)S(1)}, ...), condition=%wide.region_13.14_spmd, body=%wide.region_12.13_spmd.sunk | while | flops 131078 | bytes 786627 | solution.py:26
  359.7 1.1 bitcast_add_fusion.6
  360.8 1.1 bitcast_add_fusion.6
  361.9 1.1 bitcast_add_fusion.6
  363.0 1.1 bitcast_add_fusion.6
  364.2 1.1 bitcast_add_fusion.6
  365.3 1.1 bitcast_add_fusion.6
  366.4 1.1 bitcast_add_fusion.6
  367.5 1.1 bitcast_add_fusion.6
  368.6 1.1 bitcast_add_fusion.6
  370.8 1.1 bitcast_add_fusion.6
  371.9 1.1 bitcast_add_fusion.6
  373.0 1.1 bitcast_add_fusion.6
  374.1 1.1 bitcast_add_fusion.6
  375.2 1.1 bitcast_add_fusion.6
  376.3 1.1 bitcast_add_fusion.6
  377.4 1.1 bitcast_add_fusion.6
  378.5 1.1 bitcast_add_fusion.6
  379.7 1.1 bitcast_add_fusion.6
  380.8 1.1 bitcast_add_fusion.6
  381.9 1.1 bitcast_add_fusion.6
  383.0 1.1 bitcast_add_fusion.6
  384.1 1.1 bitcast_add_fusion.6
  385.2 1.1 bitcast_add_fusion.6
  386.3 1.1 bitcast_add_fusion.6
  387.4 1.1 bitcast_add_fusion.6
  388.5 1.1 bitcast_add_fusion.6
  389.6 1.1 bitcast_add_fusion.6
  391.8 1.1 bitcast_add_fusion.6
  392.9 1.1 bitcast_add_fusion.6
  394.0 1.1 bitcast_add_fusion.6
  395.1 1.1 bitcast_add_fusion.6
  396.3 1.1 bitcast_add_fusion.6
  397.4 1.1 bitcast_add_fusion.6
  411.7 37.3 %while.52 = (s32[]{:T(128)}, bf16[4,512,128]{2,1,0:T(8,128)(2,1)S(1)}, bf16[4,512,128]{2,1,0:T(8,128)(2,1)S(1)}, bf16[4,512,128]{2,1,0:T(8,128)(2,1)}, bf16[4,51...) while((s32[]{:T(128)}, ...), condition=%wide.region_17.18_spmd, body=%wide.region_14.17_spmd.sunk | while | flops 321522688 | bytes 5260677 | solution.py:163
  416.8 1.2 fusion.138
  418.9 1.4 fusion.140
  426.1 1.2 fusion.138
  428.2 1.4 fusion.140
  435.5 1.2 fusion.138
  437.5 1.4 fusion.140
  444.8 1.2 fusion.138
  446.8 1.4 fusion.140
  449.9 2.1 copy_bitcast_fusion
  (242 shorter events, 58.8 us)
Async XLA Ops:
  7.2 2.9 copy-start.2
  7.2 164.9 %all-gather.6.cloned.1.call-start = ((), (), s32[]{:S(2)}) async-start(), calls=%async_computation | async-start | bytes 6422528 | tf_op jit(solution)/shard_map/all_gather | solution.py:97
  8.5 2.1 copy-start.3
  10.1 1.0 copy-start.4
  43.7 101.7 %copy-start = (bf16[4,512,128]{2,1,0:T(8,128)(2,1)}, bf16[4,512,128]{2,1,0:T(8,128)(2,1)S(1)}, u32[]{:S(2)}) copy-start(bf16[4,512,128]{2,1,0:T(8,128)(2,1)S(1)} %get-tuple-element.921) | copy-start | bytes 1572868
  43.7 315.9 %all-gather.8.cloned.1.call-start = ((), (), s32[]{:S(2)}) async-start(), calls=%async_computation.1 | async-start | bytes 12845056 | tf_op jit(solution)/shard_map/all_gather | solution.py:17
  172.1 4.2 copy-start.1
Sparse Core Ops, SparseCore 0:
  43.9 128.1 all-gather.5
  210.8 148.7 all-gather.7
where the time goes:
time: 461 us; the launch traced here: 459 us
  waiting for transfers between devices  172 us (37%)
  blocking collectives  129 us (28%)
  other arithmetic  71.2 us (15%)
  matrix products  33.8 us (7%)
  local copies, waits for them, and re-layouts  25.3 us (5%)
  between operations  14.9 us (3%)
  loops' own time  12.6 us (3%)
    all_gather x1, waiting for transfers between devices, prefix(): gathered = jax.tree.map(lambda a: lax.all_gather(a, axis), part)  147 us
    unnamed x1, blocking collectives  99 us
    add x47, other arithmetic, combine(): later[0][:, None, None] * earlier[1] + later[1]  49.9 us
    psum x1, blocking collectives, per_device(): square_sum = lax.psum(square_part, 'head')  29.6 us
    all_gather x1, waiting for transfers between devices, per_device(): lax.all_gather(update[None], 'seq', axis=0, tiled=True).astype(jnp.float32)  25.4 us
  transfers between devices with their start and end apart: 2, of which 2 were waited for; matrix products, arithmetic and copies ran while one was open for 1% of the time, Pallas kernels for 0%

commit v1 on v0

v1 whole, which is shorter than its diff:
```python
import functools

import jax
import jax.numpy as jnp
from jax import lax
from jax.experimental import pallas as pl
from jax.experimental.pallas import tpu as pltpu
from jax.sharding import PartitionSpec as P

HEADS = 4
DIM = 128
TOK = 512
CH = 128
NCH = TOK // CH
XN = 4
EPS = 1e-05
MESH = pl.DeviceIdType.MESH
F32 = jnp.float32
BF16 = jnp.bfloat16
NT = (((1,), (1,)), ((), ()))
TN = (((0,), (0,)), ((), ()))


def mm(a, b, dims=None):
    if dims is None:
        return jnp.dot(a, b, preferred_element_type=F32)
    return lax.dot_general(a, b, dims, preferred_element_type=F32)


def kernel(
    zn, hn,
    q_hbm, k_hbm, v_hbm, c_hbm, ld_ref, st_ref,
    attn_hbm, gq_hbm, gk_hbm, gv_hbm,
    q, k, v, cot, attn_s, gq_s, gk_s, gv_s,
    s16, lrow, enr, ler, lb, eb, leb, bias, wt, pp, dpp, o_s, gs, qd, gkp, gvp,
    acc_s, acc_g, invb, cfb,
    cb, crx, arow, aoff, coef,
    ub, rx, tf, z1s, z1r, z2s, z2r, w3, sts, str_,
    hs_s, hs_r,
    in_sem, out_sem, c_ss, c_rs, a_ss, a_rs, u_ss, u_rs, z1_ss, z1_rs, z2_ss, z2_rs, x_ss, x_rs, h_ss, h_rs,
):
    full_width = hn * HEADS * DIM
    me = lax.axis_index("seq")
    hd = lax.axis_index("head")
    z = lax.div(me, XN)
    x = lax.rem(me, XN)
    near = [d for d in (1, 2, 3) if d < zn]
    far = [d for d in range(4, zn, 4)]

    def xdev(d):
        return {"seq": z * XN + lax.rem(x + d, XN)}

    def zdev(d):
        return {"seq": lax.rem(z + d, zn) * XN + x}

    def hdev(d):
        return {"head": lax.rem(hd + d, hn)}

    def send(src, dst, ss, rs, dev):
        return pltpu.make_async_remote_copy(
            src_ref=src, dst_ref=dst, send_sem=ss, recv_sem=rs, device_id=dev, device_id_type=MESH
        )

    loads = [
        pltpu.make_async_copy(s, d, in_sem.at[n])
        for n, (s, d) in enumerate(((k_hbm, k), (v_hbm, v), (q_hbm, q), (c_hbm, cot)))
    ]
    for copy in loads:
        copy.start()

    barrier = pltpu.get_barrier_semaphore()
    for d in range(1, XN):
        pl.semaphore_signal(barrier, inc=1, device_id=xdev(d), device_id_type=MESH)
    for d in range(1, zn):
        pl.semaphore_signal(barrier, inc=1, device_id=zdev(d), device_id_type=MESH)
    for d in range(1, hn):
        pl.semaphore_signal(barrier, inc=1, device_id=hdev(d), device_id_type=MESH)

    s16[0:HEADS, :] = ld_ref[...]
    s16[4:5, :] = st_ref[...].astype(F32)
    s16[5:8, :] = jnp.zeros((3, TOK), F32)
    sums = s16[0:8, :]
    lane = lax.broadcasted_iota(jnp.int32, (8, TOK), 1)
    shift = 1
    while shift < TOK:
        sums = sums + jnp.where(lane >= shift, pltpu.roll(sums, shift, 1), 0.0)
        shift *= 2
    lsum = sums[0:HEADS, :]
    count = sums[4:5, :]
    last = sums[:, TOK - 1 : TOK]
    enter = jnp.where(count == 0.0, jnp.exp(lsum), 0.0)
    leave = jnp.where(count == last[4:5], jnp.exp(last[0:HEADS] - lsum), 0.0)
    s16[0:8, :] = sums
    s16[8:12, :] = enter
    s16[12:16, :] = leave
    for h in range(HEADS):
        lrow[h] = lsum[h : h + 1, :]
        enr[h] = enter[h : h + 1, :]
        ler[h] = leave[h : h + 1, :]
        cb[h] = jnp.broadcast_to(enter[h : h + 1, TOK - 1 : TOK], (1, DIM))

    pl.semaphore_wait(barrier, (XN - 1) + (zn - 1) + (hn - 1))

    def c_copy(d):
        return send(cb.at[lax.rem(x + d, XN)], crx.at[x], c_ss.at[d - 1], c_rs.at[d - 1], xdev(d))

    for d in (2, 1, 3):
        c_copy(d).start()
    crx[x] = cb[x]

    def x_copy(src, dst, ss, rs, d):
        return send(src.at[lax.rem(x + d, XN)], dst.at[x], ss.at[d - 1], rs.at[d - 1], xdev(d))

    def x_arrive(src, dst, ss, rs, d):
        come = lax.rem(x + XN - d, XN)
        send(src.at[come], dst.at[come], ss.at[d - 1], rs.at[d - 1], xdev(d)).wait_recv()

    def cols(h):
        return pl.ds(pl.multiple_of(h * DIM, DIM), DIM)

    loads[0].wait()
    loads[1].wait()

    for d in (2, 1, 3, 0):
        h = lax.rem(x + d, XN)
        kt = k[:, cols(h)].astype(F32).T
        kdec = (kt * ler[h]).astype(BF16)
        ub[0, h] = mm(kdec, v[:, cols(h)]).astype(BF16)
        if d:
            x_copy(ub.at[0], rx.at[0], u_ss.at[0], u_rs.at[0], d).start()
        else:
            rx[0, h] = ub[0, h]

    for d in range(1, XN):
        come = lax.rem(x + XN - d, XN)
        send(cb.at[come], crx.at[come], c_ss.at[d - 1], c_rs.at[d - 1], xdev(d)).wait_recv()
    arow[0] = (crx[0] * crx[1]) * (crx[2] * crx[3])

    def a_copy(d):
        return send(arow.at[0], aoff.at[d - 1], a_ss.at[d - 1], a_rs.at[d - 1], zdev(d))

    for d in range(1, zn):
        a_copy(d).start()

    columns = s16[...].T
    for h in range(HEADS):
        lb[h] = jnp.broadcast_to(columns[:, h : h + 1], (TOK, DIM))
        eb[h] = jnp.broadcast_to(columns[:, 8 + h : 9 + h], (TOK, DIM))
        leb[h] = jnp.broadcast_to(columns[:, 12 + h : 13 + h], (TOK, DIM))
    row_pos = lax.broadcasted_iota(jnp.int32, (TOK, TOK), 0)
    col_pos = lax.broadcasted_iota(jnp.int32, (TOK, TOK), 1)
    inside = (row_pos >= col_pos) & (columns[:, 4:5] == s16[4:5, :])
    bias[...] = jnp.where(inside, 0.0, -1e30)
    loads[2].wait()

    def intra(h, carry):
        qt = q[:, cols(h)].astype(F32).T
        qd[h] = (qt * enr[h]).astype(BF16)
        for i in range(NCH):
            rows = slice(i * CH, (i + 1) * CH)
            wide = (i + 1) * CH
            scores = mm(q[rows, cols(h)], k[0:wide, cols(h)], NT)
            for j in range(i + 1):
                part = slice(j * CH, (j + 1) * CH)
                gap = jnp.minimum(lb[h, rows, :] - lrow[h, :, part], 0.0)
                weight = jnp.exp(gap + bias[rows, part])
                wt[h, rows, part] = weight
                pp[h, rows, part] = (scores[:, part] * weight).astype(BF16)
            o_s[rows, cols(h)] = mm(pp[h, rows, 0:wide], v[0:wide, cols(h)])
        return carry

    def row_total(n):
        if n == 0:
            total = rx[n, 0].astype(F32)
            for i in range(1, XN):
                total = total * crx[i] + rx[n, i].astype(F32)
        else:
            total = rx[n, XN - 1].astype(F32)
            for i in range(XN - 2, -1, -1):
                total = total * crx[i] + rx[n, i].astype(F32)
        return total

    def z_target(n, d):
        return zdev(d) if n == 0 else zdev(zn - d)

    def z1_copy(n, d):
        i = near.index(d)
        return send(z1s.at[n], z1r.at[n, i], z1_ss.at[n, i], z1_rs.at[n, i], z_target(n, d))

    def z2_copy(n, d):
        i = far.index(d)
        return send(z2s.at[n], z2r.at[n, i], z2_ss.at[n, i], z2_rs.at[n, i], z_target(n, d))

    def scan_start(n):
        for d in (1, 3, 2):
            x_arrive(ub.at[n], rx.at[n], u_ss.at[n], u_rs.at[n], d)
        total = row_total(n)
        tf[...] = total
        z1s[n] = total.astype(BF16)
        for d in near[::-1]:
            z1_copy(n, d).start()

    def scan_middle(n):
        window = jnp.zeros((DIM, DIM), F32)
        for d in near:
            z1_copy(n, d).wait_recv()
            window = window + coef[n, d] * z1r[n, near.index(d)].astype(F32)
        w3[...] = window
        if far:
            z2s[n] = (tf[...] + arow[0] * window).astype(BF16)
            for d in far:
                z2_copy(n, d).start()

    def scan_end(n):
        state = w3[...]
        for d in far:
            z2_copy(n, d).wait_recv()
            state = state + coef[n, d] * z2r[n, far.index(d)].astype(F32)
        order = range(XN) if n == 0 else range(XN - 1, -1, -1)
        for i in order:
            sts[n, i] = state.astype(BF16)
            state = state * crx[i] + rx[n, i].astype(F32)
        for d in (2, 1, 3):
            x_copy(sts.at[n], str_.at[n], x_ss.at[n], x_rs.at[n], d).start()
        str_[n, x] = sts[n, x]

    def state_arrive(n, d):
        if d:
            x_arrive(sts.at[n], str_.at[n], x_ss.at[n], x_rs.at[n], d)

    lax.fori_loop(0, 1, intra, 0)
    scan_start(0)
    lax.fori_loop(1, 3, intra, 0)

    for d in range(1, zn):
        a_copy(d).wait_recv()
    for n in range(2):
        product = jnp.ones((1, DIM), F32)
        for d in range(1, zn):
            ok = (z >= d) if n == 0 else (z + d < zn)
            coef[n, d] = jnp.where(ok, product, 0.0)
            product = product * (aoff[d - 1] if n == 0 else aoff[zn - d - 1])

    scan_middle(0)
    lax.fori_loop(3, HEADS, intra, 0)
    loads[3].wait()
    scan_end(0)

    for d in (0, 1, 3, 2):
        state_arrive(0, d)
        h = lax.rem(x + XN - d, XN)
        for i in range(NCH):
            rows = slice(i * CH, (i + 1) * CH)
            out = o_s[rows, cols(h)] + eb[h, rows, :] * mm(q[rows, cols(h)], str_[0, h])
            o_s[rows, cols(h)] = out
            square = out * out
            along = out * cot[rows, cols(h)].astype(F32)
            if d == 0:
                acc_s[rows, :] = square
                acc_g[rows, :] = along
            else:
                acc_s[rows, :] += square
                acc_g[rows, :] += along
    square_row = jnp.sum(acc_s[...].T, axis=0, keepdims=True)
    along_row = jnp.sum(acc_g[...].T, axis=0, keepdims=True)
    for i in range(NCH):
        hs_s[i : i + 1, :] = square_row[:, i * CH : (i + 1) * CH]
        hs_s[4 + i : 5 + i, :] = along_row[:, i * CH : (i + 1) * CH]

    def h_copy(d):
        return send(hs_s, hs_r.at[d - 1], h_ss.at[d - 1], h_rs.at[d - 1], hdev(d))

    for d in range(1, hn):
        h_copy(d).start()
    both = hs_s[...]
    for d in range(1, hn):
        h_copy(d).wait_recv()
        both = both + hs_r[d - 1]
    inverse = lax.rsqrt(both[0:4] / full_width + EPS)
    cubed = inverse * inverse * inverse
    second = cubed * both[4:8] / full_width
    flat = jnp.concatenate([inverse, second], axis=0).T
    for i in range(NCH):
        rows = slice(i * CH, (i + 1) * CH)
        invb[rows, :] = jnp.broadcast_to(flat[:, i : i + 1], (CH, DIM))
        cfb[rows, :] = jnp.broadcast_to(flat[:, 4 + i : 5 + i], (CH, DIM))

    for d in (2, 1, 3, 0):
        h = lax.rem(x + d, XN)
        for i in range(NCH):
            rows = slice(i * CH, (i + 1) * CH)
            gs[rows, cols(h)] = (
                invb[rows, :] * cot[rows, cols(h)].astype(F32) - cfb[rows, :] * o_s[rows, cols(h)]
            ).astype(BF16)
        ub[1, h] = mm(qd[h], gs[:, cols(h)]).astype(BF16)
        if d:
            x_copy(ub.at[1], rx.at[1], u_ss.at[1], u_rs.at[1], d).start()
        else:
            rx[1, h] = ub[1, h]

    def out_copy(n, h):
        src, dst = ((attn_s, attn_hbm), (gq_s, gq_hbm), (gk_s, gk_hbm), (gv_s, gv_hbm))[n]
        return pltpu.make_async_copy(src.at[:, cols(h)], dst.at[:, cols(h)], out_sem.at[n, h])

    def local_back(h, carry):
        for i in range(NCH):
            rows = slice(i * CH, (i + 1) * CH)
            wide = (i + 1) * CH
            attn_s[rows, cols(h)] = (o_s[rows, cols(h)] * invb[rows, :]).astype(BF16)
            inner = mm(gs[rows, cols(h)], v[0:wide, cols(h)], NT)
            dpp[rows, 0:wide] = (inner * wt[h, rows, 0:wide]).astype(BF16)
            grad = mm(dpp[rows, 0:wide], k[0:wide, cols(h)])
            grad = grad + eb[h, rows, :] * mm(gs[rows, cols(h)], str_[0, h], NT)
            gq_s[rows, cols(h)] = grad.astype(BF16)
        out_copy(0, h).start()
        out_copy(1, h).start()
        for j in range(NCH):
            part = slice(j * CH, (j + 1) * CH)
            gkp[part, cols(h)] = mm(dpp[j * CH :, part], q[j * CH :, cols(h)], TN)
            gvp[part, cols(h)] = mm(pp[h, j * CH :, part], gs[j * CH :, cols(h)], TN)
        return carry

    lax.fori_loop(0, 1, local_back, 0)
    scan_start(1)
    lax.fori_loop(1, 3, local_back, 0)
    scan_middle(1)
    lax.fori_loop(3, HEADS, local_back, 0)
    scan_end(1)

    for d in (0, 1, 3, 2):
        state_arrive(1, d)
        h = lax.rem(x + XN - d, XN)
        for j in range(NCH):
            part = slice(j * CH, (j + 1) * CH)
            gk_s[part, cols(h)] = (
                gkp[part, cols(h)] + leb[h, part, :] * mm(v[part, cols(h)], str_[1, h], NT)
            ).astype(BF16)
            gv_s[part, cols(h)] = (
                gvp[part, cols(h)] + leb[h, part, :] * mm(k[part, cols(h)], str_[1, h])
            ).astype(BF16)
        out_copy(2, h).start()
        out_copy(3, h).start()

    for d in range(1, XN):
        c_copy(d).wait_send()
        for n in range(2):
            x_copy(ub.at[n], rx.at[n], u_ss.at[n], u_rs.at[n], d).wait_send()
            x_copy(sts.at[n], str_.at[n], x_ss.at[n], x_rs.at[n], d).wait_send()
    for d in range(1, zn):
        a_copy(d).wait_send()
    for d in range(1, hn):
        h_copy(d).wait_send()
    for n in range(2):
        for d in near:
            z1_copy(n, d).wait_send()
        for d in far:
            z2_copy(n, d).wait_send()
    for n in range(4):
        for h in range(HEADS):
            out_copy(n, h).wait()


def solution(mesh):
    zn = mesh.shape["seq"] // XN
    hn = mesh.shape["head"]
    near = max(min(3, zn - 1), 1)
    far = max(len(range(4, zn, 4)), 1)
    dma = pltpu.SemaphoreType.DMA

    def per_device(queries, keys, values, cotangent, log_decay, starts):
        big = pltpu.VMEM((TOK, HEADS * DIM), BF16)
        bigf = pltpu.VMEM((TOK, HEADS * DIM), F32)
        col = pltpu.VMEM((HEADS, TOK, DIM), F32)
        row = pltpu.VMEM((HEADS, 1, TOK), F32)
        mat = (DIM, DIM)
        scratch = [
            big, big, big, big, big, big, big, big,
            pltpu.VMEM((16, TOK), F32), row, row, row, col, col, col,
            pltpu.VMEM((TOK, TOK), F32),
            pltpu.VMEM((HEADS, TOK, TOK), F32),
            pltpu.VMEM((HEADS, TOK, TOK), BF16),
            pltpu.VMEM((TOK, TOK), BF16),
            bigf, big, pltpu.VMEM((HEADS, DIM, TOK), BF16), bigf, bigf,
            pltpu.VMEM((TOK, DIM), F32), pltpu.VMEM((TOK, DIM), F32),
            pltpu.VMEM((TOK, DIM), F32), pltpu.VMEM((TOK, DIM), F32),
            pltpu.VMEM((HEADS, 1, DIM), F32), pltpu.VMEM((XN, 1, DIM), F32),
            pltpu.VMEM((1, 1, DIM), F32), pltpu.VMEM((max(zn - 1, 1), 1, DIM), F32),
            pltpu.VMEM((2, zn, 1, DIM), F32),
            pltpu.VMEM((2, HEADS) + mat, BF16), pltpu.VMEM((2, XN) + mat, BF16),
            pltpu.VMEM(mat, F32),
            pltpu.VMEM((2,) + mat, BF16), pltpu.VMEM((2, near) + mat, BF16),
            pltpu.VMEM((2,) + mat, BF16), pltpu.VMEM((2, far) + mat, BF16),
            pltpu.VMEM(mat, F32),
            pltpu.VMEM((2, XN) + mat, BF16), pltpu.VMEM((2, HEADS) + mat, BF16),
            pltpu.VMEM((8, DIM), F32), pltpu.VMEM((max(hn - 1, 1), 8, DIM), F32),
            dma((4,)), dma((4, HEADS)),
            dma((3,)), dma((3,)),
            dma((max(zn - 1, 1),)), dma((max(zn - 1, 1),)),
            dma((2, 3)), dma((2, 3)),
            dma((2, near)), dma((2, near)),
            dma((2, far)), dma((2, far)),
            dma((2, 3)), dma((2, 3)),
            dma((max(hn - 1, 1),)), dma((max(hn - 1, 1),)),
        ]
        out = jax.ShapeDtypeStruct(queries.shape, BF16)
        hbm = pl.BlockSpec(memory_space=pl.ANY)
        vmem = pl.BlockSpec(memory_space=pltpu.VMEM)
        return pl.pallas_call(
            functools.partial(kernel, zn, hn),
            out_shape=(out, out, out, out),
            in_specs=[hbm, hbm, hbm, hbm, vmem, vmem],
            out_specs=(hbm, hbm, hbm, hbm),
            scratch_shapes=scratch,
            compiler_params=pltpu.CompilerParams(
                collective_id=0, has_side_effects=True, vmem_limit_bytes=60 * 1024 * 1024
            ),
        )(queries, keys, values, cotangent, log_decay, starts.reshape(1, TOK))

    in_specs = (
        P("seq", "head"),
        P("seq", "head"),
        P("seq", "head"),
        P("seq", "head"),
        P("head", "seq"),
        P("seq"),
    )
    out_specs = (P("seq", "head"), P("seq", "head"), P("seq", "head"), P("seq", "head"))
    return jax.shard_map(
        per_device, mesh=mesh, in_specs=in_specs, out_specs=out_specs, check_vma=False
    )
```

time: 461 us -> 73 us (0.16)
  waiting for transfers between devices: 172 us -> 0 us
  blocking collectives: 129 us -> 0 us
  other arithmetic: 71.2 us -> 0 us
  Pallas kernels: 0 us -> 65.9 us
  matrix products: 33.8 us -> 0 us
  local copies, waits for them, and re-layouts: 25.3 us -> 5.18 us
  between operations: 14.9 us -> 0.65 us
  loops' own time: 12.6 us -> 0 us
    all_gather x2 -> x0, waiting for transfers between devices: 172 us -> none  [the longest x1 147 us: prefix(): gathered = jax.tree.map(lambda a: lax.all_gather(a, axis), part)]
    unnamed x1 -> x0, blocking collectives: 99 us -> none
    pallas_call x0 -> x1, Pallas kernels: none -> 65.9 us  [per_device(): pl.pallas_call(functools.partial(kernel, zn, hn), out_shape=(out, out, ou...]
    add x47 -> x0, other arithmetic: 49.9 us -> none  [combine(): later[0][:, None, None] * earlier[1] + later[1]]
    dot_general x42 -> x0, matrix products: 33.8 us -> none  [the longest x4 5.52 us: local_backward(): jnp.einsum('ts,td->sd', weights_rounded, grad_head, preferred_element_typ...]
    psum x1 -> x0, blocking collectives: 29.6 us -> none  [per_device(): square_sum = lax.psum(square_part, 'head')]
    another operation x3 -> x0, loops' own time: 12.6 us -> none  [the longest x1 5.49 us: per_device(): lax.map(local_forward, (query_heads, key_heads, value_heads, log_decay))]
    slice x20 -> x0, local copies, waits for them, and re-layouts: 11.7 us -> none  [the longest x12 7 us: block_factors(): cum_log[:, -1:] - cum_log]
  transfers between devices with their start and end apart: 2 -> 0, of which waited for: 2 -> 0; matrix products, arithmetic and copies ran while one was open for 1% -> 0% of each run, Pallas kernels for 0% -> 0%
where the time goes in v1:
time: 73 us; the launch traced here: 71.8 us
  Pallas kernels  65.9 us (90%)
  local copies, waits for them, and re-layouts  5.18 us (7%)
    pallas_call x1, Pallas kernels, per_device(): pl.pallas_call(functools.partial(kernel, zn, hn), out_shape=(out, out, ou...  65.9 us
    unnamed x10, local copies, waits for them, and re-layouts  5.18 us

profile of v1, /device:TPU:1, one launch (start us, length us, event | category | flops | bytes accessed | tf_op | source)
XLA Modules:
  0.0 71.8 jit_solution(5354178320108854278)
XLA Ops:
  0.6 65.9 %shard_map.93 = (bf16[512,512]{1,0:T(8,128)(2,1)}, bf16[512,512]{1,0:T(8,128)(2,1)}, bf16[512,512]{1,0:T(8,128)(2,1)}, bf16[512,512]{1,0:T(8,128)(2,1)}) custom-call(bf16[512,512]{1,0:T(8,128)(2,1)} %q_hbm.1, bf16[512,512]{1,0:T(8,128)(2,1)} %k_hbm.1, bf16[512,512]{1,0:T(8,128)(2,1)} %v_hbm.1, bf16[512,512]{1,0:T(8,128)(2,1)} %c_hbm.1, f32[4,512]{1,0:T(4,128)} %ld_ref.1, ...), custom_call_target="tpu_custom_call" | custom-call | tf_op jit(solution)/shard_map/pallas_call | solution.py:408
  66.6 0.0 copy-start.2
  66.6 1.9 %copy.14 = bf16[512,512]{1,0:T(8,128)(2,1)} copy(bf16[512,512]{1,0:T(8,128)(2,1)} %get-tuple-element.8) | data formatting | bytes 1048576
  68.5 0.0 copy-done.2
  68.5 0.0 copy-start.1
  68.5 0.8 %copy.15 = bf16[512,512]{1,0:T(8,128)(2,1)} copy(bf16[512,512]{1,0:T(8,128)(2,1)S(1)} %copy-done.2) | data formatting | bytes 1048576
  69.3 0.4 copy-done.1
  69.7 0.0 copy-start
  69.7 0.8 %copy.16 = bf16[512,512]{1,0:T(8,128)(2,1)} copy(bf16[512,512]{1,0:T(8,128)(2,1)S(1)} %copy-done.1) | data formatting | bytes 1048576
  70.5 0.4 copy-done
  71.0 0.8 %copy.17 = bf16[512,512]{1,0:T(8,128)(2,1)} copy(bf16[512,512]{1,0:T(8,128)(2,1)S(1)} %copy-done) | data formatting | bytes 1048576
Async XLA Ops:
  66.6 1.9 %copy-start.2 = (bf16[512,512]{1,0:T(8,128)(2,1)S(1)}, bf16[512,512]{1,0:T(8,128)(2,1)}, u32[]{:S(2)}) copy-start(bf16[512,512]{1,0:T(8,128)(2,1)} %get-tuple-element.9) | copy-start | bytes 1572868
  68.5 1.2 %copy-start.1 = (bf16[512,512]{1,0:T(8,128)(2,1)S(1)}, bf16[512,512]{1,0:T(8,128)(2,1)}, u32[]{:S(2)}) copy-start(bf16[512,512]{1,0:T(8,128)(2,1)} %get-tuple-element.10) | copy-start | bytes 1572868
  69.7 1.2 %copy-start = (bf16[512,512]{1,0:T(8,128)(2,1)S(1)}, bf16[512,512]{1,0:T(8,128)(2,1)}, u32[]{:S(2)}) copy-start(bf16[512,512]{1,0:T(8,128)(2,1)} %get-tuple-element.11) | copy-start | bytes 1572868

commit v2 on v1

--- a/solution.py
+++ b/solution.py
@@ -13,6 +13,8 @@
 CH = 128
 NCH = TOK // CH
 XN = 4
+PARTS = 2
+PR = DIM // PARTS
 EPS = 1e-05
 MESH = pl.DeviceIdType.MESH
 F32 = jnp.float32
@@ -29,15 +31,15 @@
 
 def kernel(
     zn, hn,
-    q_hbm, k_hbm, v_hbm, c_hbm, ld_ref, st_ref,
-    attn_hbm, gq_hbm, gk_hbm, gv_hbm,
-    q, k, v, cot, attn_s, gq_s, gk_s, gv_s,
+    q_hbm, k_hbm, v_hbm, c_hbm, ld_hbm, st_hbm,
+    attn_s, gq_s, gk_s, gv_s,
+    q, k, v, cot, ld_ref, st_ref,
     s16, lrow, enr, ler, lb, eb, leb, bias, wt, pp, dpp, o_s, gs, qd, gkp, gvp,
     acc_s, acc_g, invb, cfb,
     cb, crx, arow, aoff, coef,
     ub, rx, tf, z1s, z1r, z2s, z2r, w3, sts, str_,
     hs_s, hs_r,
-    in_sem, out_sem, c_ss, c_rs, a_ss, a_rs, u_ss, u_rs, z1_ss, z1_rs, z2_ss, z2_rs, x_ss, x_rs, h_ss, h_rs,
+    in_sem, c_ss, c_rs, a_ss, a_rs, u_ss, u_rs, z1_ss, z1_rs, z2_ss, z2_rs, x_ss, x_rs, h_ss, h_rs,
 ):
     full_width = hn * HEADS * DIM
     me = lax.axis_index("seq")
@@ -61,13 +63,6 @@
             src_ref=src, dst_ref=dst, send_sem=ss, recv_sem=rs, device_id=dev, device_id_type=MESH
         )
 
-    loads = [
-        pltpu.make_async_copy(s, d, in_sem.at[n])
-        for n, (s, d) in enumerate(((k_hbm, k), (v_hbm, v), (q_hbm, q), (c_hbm, cot)))
-    ]
-    for copy in loads:
-        copy.start()
-
     barrier = pltpu.get_barrier_semaphore()
     for d in range(1, XN):
         pl.semaphore_signal(barrier, inc=1, device_id=xdev(d), device_id_type=MESH)
@@ -76,6 +71,15 @@
     for d in range(1, hn):
         pl.semaphore_signal(barrier, inc=1, device_id=hdev(d), device_id_type=MESH)
 
+    loads = [
+        pltpu.make_async_copy(s, d, in_sem.at[n])
+        for n, (s, d) in enumerate(((ld_hbm, ld_ref), (st_hbm, st_ref), (k_hbm, k), (v_hbm, v), (q_hbm, q), (c_hbm, cot)))
+    ]
+    for copy in loads:
+        copy.start()
+
+    loads[0].wait()
+    loads[1].wait()
     s16[0:HEADS, :] = ld_ref[...]
     s16[4:5, :] = st_ref[...].astype(F32)
     s16[5:8, :] = jnp.zeros((3, TOK), F32)
@@ -108,18 +112,27 @@
         c_copy(d).start()
     crx[x] = cb[x]
 
-    def x_copy(src, dst, ss, rs, d):
-        return send(src.at[lax.rem(x + d, XN)], dst.at[x], ss.at[d - 1], rs.at[d - 1], xdev(d))
-
-    def x_arrive(src, dst, ss, rs, d):
+    def chunk(c):
+        return slice(c * PR, (c + 1) * PR)
+
+    def x_copy(src, dst, ss, rs, n, c, d):
+        return send(
+            src.at[n, lax.rem(x + d, XN), chunk(c)], dst.at[n, x, chunk(c)],
+            ss.at[n, c, d - 1], rs.at[n, c, d - 1], xdev(d),
+        )
+
+    def x_arrive(src, dst, ss, rs, n, c, d):
         come = lax.rem(x + XN - d, XN)
-        send(src.at[come], dst.at[come], ss.at[d - 1], rs.at[d - 1], xdev(d)).wait_recv()
+        send(
+            src.at[n, come, chunk(c)], dst.at[n, come, chunk(c)],
+            ss.at[n, c, d - 1], rs.at[n, c, d - 1], xdev(d),
+        ).wait_recv()
 
     def cols(h):
         return pl.ds(pl.multiple_of(h * DIM, DIM), DIM)
 
-    loads[0].wait()
-    loads[1].wait()
+    loads[2].wait()
+    loads[3].wait()
 
     for d in (2, 1, 3, 0):
         h = lax.rem(x + d, XN)
@@ -127,20 +140,12 @@
         kdec = (kt * ler[h]).astype(BF16)
         ub[0, h] = mm(kdec, v[:, cols(h)]).astype(BF16)
         if d:
-            x_copy(ub.at[0], rx.at[0], u_ss.at[0], u_rs.at[0], d).start()
+            x_copy(ub, rx, u_ss, u_rs, 0, 0, d).start()
         else:
             rx[0, h] = ub[0, h]
-
-    for d in range(1, XN):
-        come = lax.rem(x + XN - d, XN)
-        send(cb.at[come], crx.at[come], c_ss.at[d - 1], c_rs.at[d - 1], xdev(d)).wait_recv()
-    arow[0] = (crx[0] * crx[1]) * (crx[2] * crx[3])
-
-    def a_copy(d):
-        return send(arow.at[0], aoff.at[d - 1], a_ss.at[d - 1], a_rs.at[d - 1], zdev(d))
-
-    for d in range(1, zn):
-        a_copy(d).start()
+    for c in range(1, PARTS):
+        for d in (2, 1, 3):
+            x_copy(ub, rx, u_ss, u_rs, 0, c, d).start()
 
     columns = s16[...].T
     for h in range(HEADS):
@@ -151,7 +156,7 @@
     col_pos = lax.broadcasted_iota(jnp.int32, (TOK, TOK), 1)
     inside = (row_pos >= col_pos) & (columns[:, 4:5] == s16[4:5, :])
     bias[...] = jnp.where(inside, 0.0, -1e30)
-    loads[2].wait()
+    loads[4].wait()
 
     def intra(h, carry):
         qt = q[:, cols(h)].astype(F32).T
@@ -169,83 +174,108 @@
             o_s[rows, cols(h)] = mm(pp[h, rows, 0:wide], v[0:wide, cols(h)])
         return carry
 
-    def row_total(n):
-        if n == 0:
-            total = rx[n, 0].astype(F32)
-            for i in range(1, XN):
-                total = total * crx[i] + rx[n, i].astype(F32)
-        else:
-            total = rx[n, XN - 1].astype(F32)
-            for i in range(XN - 2, -1, -1):
-                total = total * crx[i] + rx[n, i].astype(F32)
+    def row_total(n, c):
+        rs = chunk(c)
+        order = range(XN) if n == 0 else range(XN - 1, -1, -1)
+        total = None
+        for i in order:
+            term = rx[n, i, rs].astype(F32)
+            total = term if total is None else total * crx[i] + term
         return total
 
     def z_target(n, d):
         return zdev(d) if n == 0 else zdev(zn - d)
 
-    def z1_copy(n, d):
+    def to_later(n, d):
+        return pl.when(z + d < zn) if n == 0 else pl.when(z >= d)
+
+    def from_earlier(n, d):
+        return pl.when(z >= d) if n == 0 else pl.when(z + d < zn)
+
+    def z1_copy(n, c, d):
         i = near.index(d)
-        return send(z1s.at[n], z1r.at[n, i], z1_ss.at[n, i], z1_rs.at[n, i], z_target(n, d))
-
-    def z2_copy(n, d):
+        return send(
+            z1s.at[n, chunk(c)], z1r.at[n, i, chunk(c)], z1_ss.at[n, c, i], z1_rs.at[n, c, i], z_target(n, d)
+        )
+
+    def z2_copy(n, c, d):
         i = far.index(d)
-        return send(z2s.at[n], z2r.at[n, i], z2_ss.at[n, i], z2_rs.at[n, i], z_target(n, d))
-
-    def scan_start(n):
+        return send(
+            z2s.at[n, chunk(c)], z2r.at[n, i, chunk(c)], z2_ss.at[n, c, i], z2_rs.at[n, c, i], z_target(n, d)
+        )
+
+    def scan_start(n, c):
         for d in (1, 3, 2):
-            x_arrive(ub.at[n], rx.at[n], u_ss.at[n], u_rs.at[n], d)
-        total = row_total(n)
-        tf[...] = total
-        z1s[n] = total.astype(BF16)
+            x_arrive(ub, rx, u_ss, u_rs, n, c, d)
+        total = row_total(n, c)
+        tf[chunk(c)] = total
+        z1s[n, chunk(c)] = total.astype(BF16)
         for d in near[::-1]:
-            z1_copy(n, d).start()
-
-    def scan_middle(n):
-        window = jnp.zeros((DIM, DIM), F32)
+            @to_later(n, d)
+            def _():
+                z1_copy(n, c, d).start()
+
+    def scan_middle(n, c):
+        w3[chunk(c)] = jnp.zeros((PR, DIM), F32)
         for d in near:
-            z1_copy(n, d).wait_recv()
-            window = window + coef[n, d] * z1r[n, near.index(d)].astype(F32)
-        w3[...] = window
+            @from_earlier(n, d)
+            def _():
+                z1_copy(n, c, d).wait_recv()
+                w3[chunk(c)] += coef[n, d] * z1r[n, near.index(d), chunk(c)].astype(F32)
         if far:
-            z2s[n] = (tf[...] + arow[0] * window).astype(BF16)
-            for d in far:
-                z2_copy(n, d).start()
-
-    def scan_end(n):
-        state = w3[...]
+            z2s[n, chunk(c)] = (tf[chunk(c)] + arow[0] * w3[chunk(c)]).astype(BF16)
         for d in far:
-            z2_copy(n, d).wait_recv()
-            state = state + coef[n, d] * z2r[n, far.index(d)].astype(F32)
+            @to_later(n, d)
+            def _():
+                z2_copy(n, c, d).start()
+
+    def scan_end(n, c):
+        for d in far:
+            @from_earlier(n, d)
+            def _():
+                z2_copy(n, c, d).wait_recv()
+                w3[chunk(c)] += coef[n, d] * z2r[n, far.index(d), chunk(c)].astype(F32)
+        state = w3[chunk(c)]
         order = range(XN) if n == 0 else range(XN - 1, -1, -1)
         for i in order:
-            sts[n, i] = state.astype(BF16)
-            state = state * crx[i] + rx[n, i].astype(F32)
+            sts[n, i, chunk(c)] = state.astype(BF16)
+            state = state * crx[i] + rx[n, i, chunk(c)].astype(F32)
         for d in (2, 1, 3):
-            x_copy(sts.at[n], str_.at[n], x_ss.at[n], x_rs.at[n], d).start()
-        str_[n, x] = sts[n, x]
+            x_copy(sts, str_, x_ss, x_rs, n, c, d).start()
+        str_[n, x, chunk(c)] = sts[n, x, chunk(c)]
 
     def state_arrive(n, d):
         if d:
-            x_arrive(sts.at[n], str_.at[n], x_ss.at[n], x_rs.at[n], d)
+            for c in range(PARTS):
+                x_arrive(sts, str_, x_ss, x_rs, n, c, d)
 
     lax.fori_loop(0, 1, intra, 0)
-    scan_start(0)
-    lax.fori_loop(1, 3, intra, 0)
-
+    for d in range(1, XN):
+        come = lax.rem(x + XN - d, XN)
+        send(cb.at[come], crx.at[come], c_ss.at[d - 1], c_rs.at[d - 1], xdev(d)).wait_recv()
+    arow[0] = (crx[0] * crx[1]) * (crx[2] * crx[3])
+
+    def a_copy(d):
+        return send(arow.at[0], aoff.at[d - 1], a_ss.at[d - 1], a_rs.at[d - 1], zdev(d))
+
+    for d in sorted(range(1, zn), key=lambda d: min(d, zn - d), reverse=True):
+        a_copy(d).start()
+
+    for c in range(PARTS):
+        scan_start(0, c)
+    lax.fori_loop(1, HEADS, intra, 0)
     for d in range(1, zn):
         a_copy(d).wait_recv()
     for n in range(2):
         product = jnp.ones((1, DIM), F32)
         for d in range(1, zn):
-            ok = (z >= d) if n == 0 else (z + d < zn)
-            coef[n, d] = jnp.where(ok, product, 0.0)
+            coef[n, d] = product
             product = product * (aoff[d - 1] if n == 0 else aoff[zn - d - 1])
-
-    scan_middle(0)
-    lax.fori_loop(3, HEADS, intra, 0)
-    loads[3].wait()
-    scan_end(0)
-
+    for c in range(PARTS):
+        scan_middle(0, c)
+    loads[5].wait()
+    for c in range(PARTS):
+        scan_end(0, c)
     for d in (0, 1, 3, 2):
         state_arrive(0, d)
         h = lax.rem(x + XN - d, XN)
@@ -270,7 +300,7 @@
     def h_copy(d):
         return send(hs_s, hs_r.at[d - 1], h_ss.at[d - 1], h_rs.at[d - 1], hdev(d))
 
-    for d in range(1, hn):
+    for d in sorted(range(1, hn), key=lambda d: min(d, hn - d), reverse=True):
         h_copy(d).start()
     both = hs_s[...]
     for d in range(1, hn):
@@ -294,13 +324,12 @@
             ).astype(BF16)
         ub[1, h] = mm(qd[h], gs[:, cols(h)]).astype(BF16)
         if d:
-            x_copy(ub.at[1], rx.at[1], u_ss.at[1], u_rs.at[1], d).start()
+            x_copy(ub, rx, u_ss, u_rs, 1, 0, d).start()
         else:
             rx[1, h] = ub[1, h]
-
-    def out_copy(n, h):
-        src, dst = ((attn_s, attn_hbm), (gq_s, gq_hbm), (gk_s, gk_hbm), (gv_s, gv_hbm))[n]
-        return pltpu.make_async_copy(src.at[:, cols(h)], dst.at[:, cols(h)], out_sem.at[n, h])
+    for c in range(1, PARTS):
+        for d in (2, 1, 3):
+            x_copy(ub, rx, u_ss, u_rs, 1, c, d).start()
 
     def local_back(h, carry):
         for i in range(NCH):
@@ -312,21 +341,20 @@
             grad = mm(dpp[rows, 0:wide], k[0:wide, cols(h)])
             grad = grad + eb[h, rows, :] * mm(gs[rows, cols(h)], str_[0, h], NT)
             gq_s[rows, cols(h)] = grad.astype(BF16)
-        out_copy(0, h).start()
-        out_copy(1, h).start()
         for j in range(NCH):
             part = slice(j * CH, (j + 1) * CH)
             gkp[part, cols(h)] = mm(dpp[j * CH :, part], q[j * CH :, cols(h)], TN)
             gvp[part, cols(h)] = mm(pp[h, j * CH :, part], gs[j * CH :, cols(h)], TN)
         return carry
 
-    lax.fori_loop(0, 1, local_back, 0)
-    scan_start(1)
-    lax.fori_loop(1, 3, local_back, 0)
-    scan_middle(1)
-    lax.fori_loop(3, HEADS, local_back, 0)
-    scan_end(1)
-
+    lax.fori_loop(0, 2, local_back, 0)
+    for c in range(PARTS):
+        scan_start(1, c)
+    lax.fori_loop(2, HEADS, local_back, 0)
+    for c in range(PARTS):
+        scan_middle(1, c)
+    for c in range(PARTS):
+        scan_end(1, c)
     for d in (0, 1, 3, 2):
         state_arrive(1, d)
         h = lax.rem(x + XN - d, XN)
@@ -338,26 +366,33 @@
             gv_s[part, cols(h)] = (
                 gvp[part, cols(h)] + leb[h, part, :] * mm(k[part, cols(h)], str_[1, h])
             ).astype(BF16)
-        out_copy(2, h).start()
-        out_copy(3, h).start()
 
     for d in range(1, XN):
         c_copy(d).wait_send()
         for n in range(2):
-            x_copy(ub.at[n], rx.at[n], u_ss.at[n], u_rs.at[n], d).wait_send()
-            x_copy(sts.at[n], str_.at[n], x_ss.at[n], x_rs.at[n], d).wait_send()
+            for c in range(PARTS):
+                x_copy(ub, rx, u_ss, u_rs, n, c, d).wait_send()
+                x_copy(sts, str_, x_ss, x_rs, n, c, d).wait_send()
     for d in range(1, zn):
         a_copy(d).wait_send()
     for d in range(1, hn):
         h_copy(d).wait_send()
     for n in range(2):
-        for d in near:
-            z1_copy(n, d).wait_send()
-        for d in far:
-            z2_copy(n, d).wait_send()
-    for n in range(4):
-        for h in range(HEADS):
-            out_copy(n, h).wait()
+        for copy, steps in ((z1_copy, near), (z2_copy, far)):
+            for d in steps:
+                @to_later(n, d)
+                def _():
+                    for c in range(PARTS):
+                        copy(n, c, d).wait_send()
+
+
+def store_kernel(*refs):
+    sem = refs[-1]
+    copies = [pltpu.make_async_copy(refs[n], refs[4 + n], sem.at[n]) for n in range(4)]
+    for copy in copies:
+        copy.start()
+    for copy in copies:
+        copy.wait()
 
 
 def solution(mesh):
@@ -374,7 +409,7 @@
         row = pltpu.VMEM((HEADS, 1, TOK), F32)
         mat = (DIM, DIM)
         scratch = [
-            big, big, big, big, big, big, big, big,
+            big, big, big, big, pltpu.VMEM((HEADS, TOK), F32), pltpu.VMEM((1, TOK), jnp.int32),
             pltpu.VMEM((16, TOK), F32), row, row, row, col, col, col,
             pltpu.VMEM((TOK, TOK), F32),
             pltpu.VMEM((HEADS, TOK, TOK), F32),
@@ -393,28 +428,36 @@
             pltpu.VMEM(mat, F32),
             pltpu.VMEM((2, XN) + mat, BF16), pltpu.VMEM((2, HEADS) + mat, BF16),
             pltpu.VMEM((8, DIM), F32), pltpu.VMEM((max(hn - 1, 1), 8, DIM), F32),
-            dma((4,)), dma((4, HEADS)),
+            dma((6,)),
             dma((3,)), dma((3,)),
             dma((max(zn - 1, 1),)), dma((max(zn - 1, 1),)),
-            dma((2, 3)), dma((2, 3)),
-            dma((2, near)), dma((2, near)),
-            dma((2, far)), dma((2, far)),
-            dma((2, 3)), dma((2, 3)),
+            dma((2, PARTS, 3)), dma((2, PARTS, 3)),
+            dma((2, PARTS, near)), dma((2, PARTS, near)),
+            dma((2, PARTS, far)), dma((2, PARTS, far)),
+            dma((2, PARTS, 3)), dma((2, PARTS, 3)),
             dma((max(hn - 1, 1),)), dma((max(hn - 1, 1),)),
         ]
         out = jax.ShapeDtypeStruct(queries.shape, BF16)
+        kept = pltpu.VMEM(queries.shape, BF16)
         hbm = pl.BlockSpec(memory_space=pl.ANY)
         vmem = pl.BlockSpec(memory_space=pltpu.VMEM)
-        return pl.pallas_call(
+        results = pl.pallas_call(
             functools.partial(kernel, zn, hn),
-            out_shape=(out, out, out, out),
-            in_specs=[hbm, hbm, hbm, hbm, vmem, vmem],
-            out_specs=(hbm, hbm, hbm, hbm),
+            out_shape=(kept,) * 4,
+            in_specs=[hbm] * 6,
+            out_specs=(vmem,) * 4,
             scratch_shapes=scratch,
             compiler_params=pltpu.CompilerParams(
                 collective_id=0, has_side_effects=True, vmem_limit_bytes=60 * 1024 * 1024
             ),
         )(queries, keys, values, cotangent, log_decay, starts.reshape(1, TOK))
+        return pl.pallas_call(
+            store_kernel,
+            out_shape=(out,) * 4,
+            in_specs=[vmem] * 4,
+            out_specs=(hbm,) * 4,
+            scratch_shapes=[dma((4,))],
+        )(*[pltpu.with_memory_space_constraint(r, pltpu.VMEM) for r in results])
 
     in_specs = (
         P("seq", "head"),

time: 73 us -> 66.7 us (0.914)
  local copies, waits for them, and re-layouts: 5.18 us -> 0 us
    unnamed x10 -> x0, local copies, waits for them, and re-layouts: 5.18 us -> none
    pallas_call x1 -> x2, Pallas kernels: 65.9 us -> 65.2 us  [the longest x1 63.8 us: per_device(): pl.pallas_call(functools.partial(kernel, zn, hn), out_shape=(kept,) * 4,...]
where the time goes in v2:
time: 66.7 us; the launch traced here: 65.8 us
  Pallas kernels  65.2 us (98%)
    pallas_call x1, Pallas kernels, per_device(): pl.pallas_call(functools.partial(kernel, zn, hn), out_shape=(kept,) * 4,...  63.8 us
    pallas_call x1, Pallas kernels, per_device(): pl.pallas_call(store_kernel, out_shape=(out,) * 4, in_specs=[vmem] * 4, o...  1.35 us

profile of v2, /device:TPU:1, one launch (start us, length us, event | category | flops | bytes accessed | tf_op | source)
XLA Modules:
  0.0 65.8 jit_solution(10309278038754323392)
XLA Ops:
  0.6 63.8 %shard_map.93 = (bf16[512,512]{1,0:T(8,128)(2,1)S(1)}, bf16[512,512]{1,0:T(8,128)(2,1)S(1)}, bf16[512,512]{1,0:T(8,128)(2,1)S(1)}, bf16[512,512]{1,0:T(8,128)(2,1)S(1)}) custom-call(bf16[512,512]{1,0:T(8,128)(2,1)} %q_hbm.1, bf16[512,512]{1,0:T(8,128)(2,1)} %k_hbm.1, bf16[512,512]{1,0:T(8,128)(2,1)} %v_hbm.1, bf16[512,512]{1,0:T(8,128)(2,1)} %c_hbm.1, ...), custom_call_target="tpu_custom_call" | custom-call | tf_op jit(solution)/shard_map/pallas_call | solution.py:444
  64.5 1.3 %shard_map.94 = (bf16[512,512]{1,0:T(8,128)(2,1)}, bf16[512,512]{1,0:T(8,128)(2,1)}, bf16[512,512]{1,0:T(8,128)(2,1)}, bf16[512,512]{1,0:T(8,128)(2,1)}) custom-call(bf16[512,512]{1,0:T(8,128)(2,1)S(1)} %get-tuple-element.8.refs_0_, bf16[512,512]{1,0:T(8,128)(2,1)S(1)} %get-tuple-element.9.refs_1_, bf16[512,512]{1,0:T(8,128)(2,1)S(1)} %get-tuple-element.10.refs_2_, ...), custom_call_target="tpu_custom_call" | custom-call | tf_op jit(solution)/shard_map/pallas_call | solution.py:454

commit v3 on v2

--- a/solution.py
+++ b/solution.py
@@ -36,10 +36,10 @@
     q, k, v, cot, ld_ref, st_ref,
     s16, lrow, enr, ler, lb, eb, leb, bias, wt, pp, dpp, o_s, gs, qd, gkp, gvp,
     acc_s, acc_g, invb, cfb,
-    cb, crx, arow, aoff, coef,
+    cb, crx, arow, a1r, aw, a2r, cf, coef,
     ub, rx, tf, z1s, z1r, z2s, z2r, w3, sts, str_,
     hs_s, hs_r,
-    in_sem, c_ss, c_rs, a_ss, a_rs, u_ss, u_rs, z1_ss, z1_rs, z2_ss, z2_rs, x_ss, x_rs, h_ss, h_rs,
+    in_sem, c_ss, c_rs, a1_ss, a1_rs, a2_ss, a2_rs, u_ss, u_rs, z1_ss, z1_rs, z2_ss, z2_rs, x_ss, x_rs, h_ss, h_rs,
 ):
     full_width = hn * HEADS * DIM
     me = lax.axis_index("seq")
@@ -64,19 +64,36 @@
         )
 
     barrier = pltpu.get_barrier_semaphore()
-    for d in range(1, XN):
-        pl.semaphore_signal(barrier, inc=1, device_id=xdev(d), device_id_type=MESH)
-    for d in range(1, zn):
-        pl.semaphore_signal(barrier, inc=1, device_id=zdev(d), device_id_type=MESH)
-    for d in range(1, hn):
-        pl.semaphore_signal(barrier, inc=1, device_id=hdev(d), device_id_type=MESH)
-
+
+    def greet(dev):
+        pl.semaphore_signal(barrier, inc=1, device_id=dev, device_id_type=MESH)
+
+    def to_later(n, d):
+        return pl.when(z + d < zn) if n == 0 else pl.when(z >= d)
+
+    def from_earlier(n, d):
+        return pl.when(z >= d) if n == 0 else pl.when(z + d < zn)
+
+    def z_target(n, d):
+        return zdev(d) if n == 0 else zdev(zn - d)
+
+    for n in (1, 0):
+        for d in (far + near[::-1]):
+            @to_later(n, d)
+            def _():
+                greet(z_target(n, d))
     loads = [
         pltpu.make_async_copy(s, d, in_sem.at[n])
-        for n, (s, d) in enumerate(((ld_hbm, ld_ref), (st_hbm, st_ref), (k_hbm, k), (v_hbm, v), (q_hbm, q), (c_hbm, cot)))
+        for n, (s, d) in enumerate(
+            ((ld_hbm, ld_ref), (st_hbm, st_ref), (k_hbm, k), (v_hbm, v), (q_hbm, q), (c_hbm, cot))
+        )
     ]
     for copy in loads:
         copy.start()
+    for d in range(1, XN):
+        greet(xdev(d))
+    for d in range(1, hn):
+        greet(hdev(d))
 
     loads[0].wait()
     loads[1].wait()
@@ -103,14 +120,9 @@
         ler[h] = leave[h : h + 1, :]
         cb[h] = jnp.broadcast_to(enter[h : h + 1, TOK - 1 : TOK], (1, DIM))
 
-    pl.semaphore_wait(barrier, (XN - 1) + (zn - 1) + (hn - 1))
-
     def c_copy(d):
         return send(cb.at[lax.rem(x + d, XN)], crx.at[x], c_ss.at[d - 1], c_rs.at[d - 1], xdev(d))
 
-    for d in (2, 1, 3):
-        c_copy(d).start()
-    crx[x] = cb[x]
 
     def chunk(c):
         return slice(c * PR, (c + 1) * PR)
@@ -133,20 +145,22 @@
 
     loads[2].wait()
     loads[3].wait()
-
     for d in (2, 1, 3, 0):
         h = lax.rem(x + d, XN)
         kt = k[:, cols(h)].astype(F32).T
         kdec = (kt * ler[h]).astype(BF16)
         ub[0, h] = mm(kdec, v[:, cols(h)]).astype(BF16)
-        if d:
-            x_copy(ub, rx, u_ss, u_rs, 0, 0, d).start()
-        else:
-            rx[0, h] = ub[0, h]
-    for c in range(1, PARTS):
+    peers = (XN - 1) + (hn - 1)
+    for d in near + far:
+        peers = peers + lax.div(z + zn - d, zn) + lax.div(2 * zn - 1 - z - d, zn)
+    pl.semaphore_wait(barrier, peers)
+    for d in (2, 1, 3):
+        c_copy(d).start()
+    for c in range(PARTS):
         for d in (2, 1, 3):
             x_copy(ub, rx, u_ss, u_rs, 0, c, d).start()
-
+    crx[x] = cb[x]
+    rx[0, x] = ub[0, x]
     columns = s16[...].T
     for h in range(HEADS):
         lb[h] = jnp.broadcast_to(columns[:, h : h + 1], (TOK, DIM))
@@ -183,14 +197,13 @@
             total = term if total is None else total * crx[i] + term
         return total
 
-    def z_target(n, d):
-        return zdev(d) if n == 0 else zdev(zn - d)
-
-    def to_later(n, d):
-        return pl.when(z + d < zn) if n == 0 else pl.when(z >= d)
-
-    def from_earlier(n, d):
-        return pl.when(z >= d) if n == 0 else pl.when(z + d < zn)
+    def a1_copy(n, d):
+        i = near.index(d)
+        return send(arow.at[0], a1r.at[n, i], a1_ss.at[n, i], a1_rs.at[n, i], z_target(n, d))
+
+    def a2_copy(n, d):
+        i = far.index(d)
+        return send(aw.at[n], a2r.at[n, i], a2_ss.at[n, i], a2_rs.at[n, i], z_target(n, d))
 
     def z1_copy(n, c, d):
         i = near.index(d)
@@ -217,22 +230,36 @@
 
     def scan_middle(n, c):
         w3[chunk(c)] = jnp.zeros((PR, DIM), F32)
+        if c == 0:
+            cf[n] = jnp.ones((1, DIM), F32)
         for d in near:
             @from_earlier(n, d)
             def _():
+                if c == 0:
+                    a1_copy(n, d).wait_recv()
+                    coef[n, d] = cf[n]
+                    cf[n] = cf[n] * a1r[n, near.index(d)]
                 z1_copy(n, c, d).wait_recv()
                 w3[chunk(c)] += coef[n, d] * z1r[n, near.index(d), chunk(c)].astype(F32)
         if far:
+            if c == 0:
+                aw[n] = arow[0] * cf[n]
             z2s[n, chunk(c)] = (tf[chunk(c)] + arow[0] * w3[chunk(c)]).astype(BF16)
         for d in far:
             @to_later(n, d)
             def _():
+                if c == 0:
+                    a2_copy(n, d).start()
                 z2_copy(n, c, d).start()
 
     def scan_end(n, c):
         for d in far:
             @from_earlier(n, d)
             def _():
+                if c == 0:
+                    a2_copy(n, d).wait_recv()
+                    coef[n, d] = cf[n]
+                    cf[n] = cf[n] * a2r[n, far.index(d)]
                 z2_copy(n, c, d).wait_recv()
                 w3[chunk(c)] += coef[n, d] * z2r[n, far.index(d), chunk(c)].astype(F32)
         state = w3[chunk(c)]
@@ -255,22 +282,14 @@
         send(cb.at[come], crx.at[come], c_ss.at[d - 1], c_rs.at[d - 1], xdev(d)).wait_recv()
     arow[0] = (crx[0] * crx[1]) * (crx[2] * crx[3])
 
-    def a_copy(d):
-        return send(arow.at[0], aoff.at[d - 1], a_ss.at[d - 1], a_rs.at[d - 1], zdev(d))
-
-    for d in sorted(range(1, zn), key=lambda d: min(d, zn - d), reverse=True):
-        a_copy(d).start()
-
+    for n in range(2):
+        for d in near:
+            @to_later(n, d)
+            def _():
+                a1_copy(n, d).start()
     for c in range(PARTS):
         scan_start(0, c)
     lax.fori_loop(1, HEADS, intra, 0)
-    for d in range(1, zn):
-        a_copy(d).wait_recv()
-    for n in range(2):
-        product = jnp.ones((1, DIM), F32)
-        for d in range(1, zn):
-            coef[n, d] = product
-            product = product * (aoff[d - 1] if n == 0 else aoff[zn - d - 1])
     for c in range(PARTS):
         scan_middle(0, c)
     loads[5].wait()
@@ -373,22 +392,25 @@
             for c in range(PARTS):
                 x_copy(ub, rx, u_ss, u_rs, n, c, d).wait_send()
                 x_copy(sts, str_, x_ss, x_rs, n, c, d).wait_send()
-    for d in range(1, zn):
-        a_copy(d).wait_send()
     for d in range(1, hn):
         h_copy(d).wait_send()
     for n in range(2):
-        for copy, steps in ((z1_copy, near), (z2_copy, far)):
+        for copy, small, steps in ((z1_copy, a1_copy, near), (z2_copy, a2_copy, far)):
             for d in steps:
                 @to_later(n, d)
                 def _():
+                    small(n, d).wait_send()
                     for c in range(PARTS):
                         copy(n, c, d).wait_send()
 
 
 def store_kernel(*refs):
     sem = refs[-1]
-    copies = [pltpu.make_async_copy(refs[n], refs[4 + n], sem.at[n]) for n in range(4)]
+    copies = [
+        pltpu.make_async_copy(refs[n].at[pl.ds(i * CH, CH)], refs[4 + n].at[pl.ds(i * CH, CH)], sem.at[n, i])
+        for n in range(4)
+        for i in range(NCH)
+    ]
     for copy in copies:
         copy.start()
     for copy in copies:
@@ -419,7 +441,9 @@
             pltpu.VMEM((TOK, DIM), F32), pltpu.VMEM((TOK, DIM), F32),
             pltpu.VMEM((TOK, DIM), F32), pltpu.VMEM((TOK, DIM), F32),
             pltpu.VMEM((HEADS, 1, DIM), F32), pltpu.VMEM((XN, 1, DIM), F32),
-            pltpu.VMEM((1, 1, DIM), F32), pltpu.VMEM((max(zn - 1, 1), 1, DIM), F32),
+            pltpu.VMEM((1, 1, DIM), F32), pltpu.VMEM((2, near, 1, DIM), F32),
+            pltpu.VMEM((2, 1, DIM), F32), pltpu.VMEM((2, far, 1, DIM), F32),
+            pltpu.VMEM((2, 1, DIM), F32),
             pltpu.VMEM((2, zn, 1, DIM), F32),
             pltpu.VMEM((2, HEADS) + mat, BF16), pltpu.VMEM((2, XN) + mat, BF16),
             pltpu.VMEM(mat, F32),
@@ -430,7 +454,8 @@
             pltpu.VMEM((8, DIM), F32), pltpu.VMEM((max(hn - 1, 1), 8, DIM), F32),
             dma((6,)),
             dma((3,)), dma((3,)),
-            dma((max(zn - 1, 1),)), dma((max(zn - 1, 1),)),
+            dma((2, near)), dma((2, near)),
+            dma((2, far)), dma((2, far)),
             dma((2, PARTS, 3)), dma((2, PARTS, 3)),
             dma((2, PARTS, near)), dma((2, PARTS, near)),
             dma((2, PARTS, far)), dma((2, PARTS, far)),
@@ -456,7 +481,7 @@
             out_shape=(out,) * 4,
             in_specs=[vmem] * 4,
             out_specs=(hbm,) * 4,
-            scratch_shapes=[dma((4,))],
+            scratch_shapes=[dma((4, NCH))],
         )(*[pltpu.with_memory_space_constraint(r, pltpu.VMEM) for r in results])
 
     in_specs = (

time: 66.7 us -> 67.2 us (level)
  the two profiles are of different devices: /device:TPU:1 before, /device:TPU:64 now
where the time goes in v3:
time: 67.2 us; the launch traced here: 67.1 us
  Pallas kernels  66.4 us (99%)
    pallas_call x1, Pallas kernels, per_device(): pl.pallas_call(functools.partial(kernel, zn, hn), out_shape=(kept,) * 4,...  65 us
    pallas_call x1, Pallas kernels, per_device(): pl.pallas_call(store_kernel, out_shape=(out,) * 4, in_specs=[vmem] * 4, o...  1.44 us

profile of v3, /device:TPU:64, one launch (start us, length us, event | category | flops | bytes accessed | tf_op | source)
XLA Modules:
  0.0 67.1 jit_solution(4222013260902737454)
XLA Ops:
  0.6 65.0 %shard_map.93 = (bf16[512,512]{1,0:T(8,128)(2,1)S(1)}, bf16[512,512]{1,0:T(8,128)(2,1)S(1)}, bf16[512,512]{1,0:T(8,128)(2,1)S(1)}, bf16[512,512]{1,0:T(8,128)(2,1)S(1)}) custom-call(bf16[512,512]{1,0:T(8,128)(2,1)} %q_hbm.1, bf16[512,512]{1,0:T(8,128)(2,1)} %k_hbm.1, bf16[512,512]{1,0:T(8,128)(2,1)} %v_hbm.1, bf16[512,512]{1,0:T(8,128)(2,1)} %c_hbm.1, ...), custom_call_target="tpu_custom_call" | custom-call | tf_op jit(solution)/shard_map/pallas_call | solution.py:469
  65.6 1.4 %shard_map.94 = (bf16[512,512]{1,0:T(8,128)(2,1)}, bf16[512,512]{1,0:T(8,128)(2,1)}, bf16[512,512]{1,0:T(8,128)(2,1)}, bf16[512,512]{1,0:T(8,128)(2,1)}) custom-call(bf16[512,512]{1,0:T(8,128)(2,1)S(1)} %get-tuple-element.8.refs_0_, bf16[512,512]{1,0:T(8,128)(2,1)S(1)} %get-tuple-element.9.refs_1_, bf16[512,512]{1,0:T(8,128)(2,1)S(1)} %get-tuple-element.10.refs_2_, ...), custom_call_target="tpu_custom_call" | custom-call | tf_op jit(solution)/shard_map/pallas_call | solution.py:479
